TPU v7x, 32 devices: a whole 2x2x4 slice. The times are simulated.
32 devices in a mesh: parts: 1, tile: 16 (over z, y, core), face: 2 (over x), sub: 1.
Axes of the slice: x: 2, y: 2, z: 4, core: 2. Of those that a mesh axis runs over, the one named last changes fastest.
Arguments:
- fields: bfloat16 [96, 4, 32, 96], P('sub', 'face', 'tile', 'parts'), may hold values from -6 to 6
- upstream: bfloat16 [96, 4, 32, 96], P('sub', 'face', 'tile', 'parts'), may hold values from -6 to 6
- kernel_one: bfloat16 [3, 3, 96, 96], replicated, may hold values from -0.21875 to 0.21875
- kernel_two: bfloat16 [3, 3, 96, 96], replicated, may hold values from -0.21875 to 0.21875
Outputs:
- result: bfloat16 [96, 4, 32, 96], P('sub', 'face', 'tile', 'parts')
- fields_grad: bfloat16 [96, 4, 32, 96], P('sub', 'face', 'tile', 'parts')
- kernel_one_grad: float32 [3, 3, 96, 96], P('parts', None, None, 'sub')
- kernel_two_grad: float32 [3, 3, 96, 96], P('parts', None, None, 'sub')
All inputs are finite; a program needn't handle non-finite values.
Results may differ from a plain program's by a relative error of at most 0.0049.
Values may be sent and summed in bfloat16 or wider, within the bound.
A program may use at most 128 MiB of HBM per device.

v0:
```python
import functools

import jax
import jax.numpy as jnp
from jax import lax
from jax.experimental import pallas as pl
from jax.experimental.pallas import tpu as pltpu
from jax.sharding import PartitionSpec as P

MESH = pl.DeviceIdType.MESH
F32 = jnp.float32
BF16 = jnp.bfloat16


def gelu_parts(v):
    root = 0.7978845608028654
    cube = 0.044715 * (v * v * v)
    th = jnp.tanh(root * (v + cube))
    value = v * (0.5 * (1.0 + th))
    slope = 0.5 * (1.0 + th) + 0.5 * v * (1.0 - th * th) * root * (1.0 + 0.134145 * (v * v))
    return value, slope


def product(a, b, da, db):
    return lax.dot_general(a, b, (((da,), (db,)), ((), ())), preferred_element_type=F32)


def body(n_t, n_f, scale, x, k1, k2, res_o, fg_o, w1_o, w2_o,
         y, rows, lh, rh, ap, bm, tr, dr, tl, dl, pad, xb, xf1, xf2,
         acc, sbuf, rbuf, obuf,
         col_s, col_r, a_s, a_r, b_s, b_r, t_s, t_r, d_s, d_r, w_s, w_r):
    _, G, J, H, C = x.shape
    S = H // 3
    W = S + 16
    M = G * J * H
    t = lax.axis_index("tile")
    f = lax.axis_index("face")
    fn = lax.rem(f + 1, n_f)
    fp = lax.rem(f + n_f - 1, n_f)
    first = t == 0
    last = t == n_t - 1

    def where_to(tile, face):
        return {"tile": tile, "face": face}

    def remote(src, dst, s, r, dev):
        return pltpu.make_async_remote_copy(
            src_ref=src, dst_ref=dst, send_sem=s, recv_sem=r, device_id=dev, device_id_type=MESH)

    def stage_rows(p, src):
        for u in range(2):
            for q in range(G):
                for j in range(J):
                    v = src[u, q, j].astype(F32)
                    rows[p, 0, u, q, j:j + 1, :] = v[0:1]
                    rows[p, 1, u, q, j:j + 1, :] = v[H - 1:H]

    def copies(p, src):
        c0, cl = src.at[:, :, 0], src.at[:, :, J - 1]
        right = lambda: remote(cl, lh.at[p], col_s.at[p, 0], col_r.at[p, 0], where_to(jnp.minimum(t + 1, n_t - 1), f))
        left = lambda: remote(c0, rh.at[p], col_s.at[p, 1], col_r.at[p, 1], where_to(jnp.maximum(t - 1, 0), f))
        seam = []
        if G > 1:
            seam.append((first, lambda: remote(src.at[:, 1:G, 0], rh.at[p, :, 0:G - 1], col_s.at[p, 2], col_r.at[p, 2], where_to(n_t - 1, f))))
            seam.append((last, lambda: remote(src.at[:, 0:G - 1, J - 1], lh.at[p, :, 1:G], col_s.at[p, 3], col_r.at[p, 3], where_to(0, f))))
        seam.append((first, lambda: remote(src.at[:, 0:1, 0], rh.at[p, :, G - 1:G], col_s.at[p, 4], col_r.at[p, 4], where_to(n_t - 1, fp))))
        seam.append((last, lambda: remote(src.at[:, G - 1:G, J - 1], lh.at[p, :, 0:1], col_s.at[p, 5], col_r.at[p, 5], where_to(0, fn))))
        a_own = lambda d: remote(src.at[:, 1:G, 0, 0:W], ap.at[p, :, 0:G - 1], a_s.at[p, 0, d], a_r.at[p, 0], where_to(d, f))
        a_oth = lambda d: remote(src.at[:, 0:1, 0, 0:W], ap.at[p, :, G - 1:G], a_s.at[p, 1, d], a_r.at[p, 1], where_to(d, fp))
        b_own = lambda d: remote(src.at[:, 0:G - 1, J - 1, H - W:H], bm.at[p, :, 1:G], b_s.at[p, 0, d], b_r.at[p, 0], where_to(d, f))
        b_oth = lambda d: remote(src.at[:, G - 1:G, J - 1, H - W:H], bm.at[p, :, 0:1], b_s.at[p, 1, d], b_r.at[p, 1], where_to(d, fn))
        t_own = lambda d: remote(rows.at[p, 0, :, 0:G - 1], tr.at[p, d, :, 1:G], t_s.at[p, 0], t_r.at[p, 0, d], where_to(0, f))
        t_oth = lambda d: remote(rows.at[p, 0, :, G - 1:G], tr.at[p, d, :, 0:1], t_s.at[p, 1], t_r.at[p, 1, d], where_to(0, fn))
        d_own = lambda d: remote(rows.at[p, 1, :, 1:G], dr.at[p, d, :, 0:G - 1], d_s.at[p, 0], d_r.at[p, 0, d], where_to(n_t - 1, f))
        d_oth = lambda d: remote(rows.at[p, 1, :, 0:1], dr.at[p, d, :, G - 1:G], d_s.at[p, 1], d_r.at[p, 1, d], where_to(n_t - 1, fp))
        return right, left, seam, a_own, a_oth, b_own, b_oth, t_own, t_oth, d_own, d_oth

    def start(p, src):
        right, left, seam, a_own, a_oth, b_own, b_oth, t_own, t_oth, d_own, d_oth = copies(p, src)

        @pl.when(jnp.logical_not(last))
        def _():
            right().start()

        @pl.when(jnp.logical_not(first))
        def _():
            left().start()

        for cond, make in seam:
            @pl.when(cond)
            def _(make=make):
                make().start()

        t_oth(t).start()
        d_oth(t).start()

        @pl.when(first)
        def _():
            if G > 1:
                @pl.loop(1, n_t)
                def _(d):
                    a_own(d).start()
                ap[p, :, 0:G - 1] = src[:, 1:G, 0, 0:W]
                tr[p, 0, :, 1:G] = rows[p, 0, :, 0:G - 1]

            @pl.loop(0, n_t)
            def _(d):
                a_oth(d).start()

        @pl.when(last)
        def _():
            if G > 1:
                @pl.loop(0, n_t - 1)
                def _(d):
                    b_own(d).start()
                bm[p, :, 1:G] = src[:, 0:G - 1, J - 1, H - W:H]
                dr[p, n_t - 1, :, 0:G - 1] = rows[p, 1, :, 1:G]

            @pl.loop(0, n_t)
            def _(d):
                b_oth(d).start()

        if G > 1:
            @pl.when(jnp.logical_not(first))
            def _():
                t_own(t).start()

            @pl.when(jnp.logical_not(last))
            def _():
                d_own(t).start()

    def await_arrivals(p, src):
        right, left, seam, a_own, a_oth, b_own, b_oth, t_own, t_oth, d_own, d_oth = copies(p, src)

        @pl.when(jnp.logical_not(first))
        def _():
            right().wait_recv()
            if G > 1:
                a_own(0).wait_recv()

        @pl.when(jnp.logical_not(last))
        def _():
            left().wait_recv()
            if G > 1:
                b_own(0).wait_recv()

        for cond, make in seam:
            other = last if cond is first else first

            @pl.when(other)
            def _(make=make):
                make().wait_recv()

        a_oth(0).wait_recv()
        b_oth(0).wait_recv()

        @pl.when(first)
        def _():
            if G > 1:
                @pl.loop(1, n_t)
                def _(d):
                    t_own(d).wait_recv()

            @pl.loop(0, n_t)
            def _(d):
                t_oth(d).wait_recv()
            for d in range(n_t):
                tl[:, :, 8 + d * J:8 + (d + 1) * J, :] = tr[p, d]

        @pl.when(last)
        def _():
            if G > 1:
                @pl.loop(0, n_t - 1)
                def _(d):
                    d_own(d).wait_recv()

            @pl.loop(0, n_t)
            def _(d):
                d_oth(d).wait_recv()
            for d in range(n_t):
                dl[:, :, 8 + d * J:8 + (d + 1) * J, :] = dr[p, d]

    def await_sends(p, src):
        right, left, seam, a_own, a_oth, b_own, b_oth, t_own, t_oth, d_own, d_oth = copies(p, src)

        @pl.when(jnp.logical_not(last))
        def _():
            right().wait_send()
            if G > 1:
                d_own(t).wait_send()

        @pl.when(jnp.logical_not(first))
        def _():
            left().wait_send()
            if G > 1:
                t_own(t).wait_send()

        for cond, make in seam:
            @pl.when(cond)
            def _(make=make):
                make().wait_send()
        t_oth(t).wait_send()
        d_oth(t).wait_send()

        @pl.when(first)
        def _():
            if G > 1:
                @pl.loop(1, n_t)
                def _(d):
                    a_own(d).wait_send()

            @pl.loop(0, n_t)
            def _(d):
                a_oth(d).wait_send()

        @pl.when(last)
        def _():
            if G > 1:
                @pl.loop(0, n_t - 1)
                def _(d):
                    b_own(d).wait_send()

            @pl.loop(0, n_t)
            def _(d):
                b_oth(d).wait_send()

    spot = lax.broadcasted_iota(jnp.int32, (8, W), 0) + (t * J - 1)
    lane = lax.broadcasted_iota(jnp.int32, (8, W), 1)
    spread_a = spot == lane
    spread_b = spot + 16 == lane

    def one_hot(mask):
        return jnp.where(mask, 1.0, 0.0).astype(BF16)

    def fill_columns(u, src):
        for q in range(G):
            for j in range(J):
                pad[q, 1 + j, 8:8 + H, :] = src[u, q, j].astype(F32)

    def forward_taps(p, src, out):
        fill_columns(0, src)
        for q in range(G):
            @pl.when(jnp.logical_not(first))
            def _():
                pad[q, 0, 8:8 + H, :] = lh[p, 0, q].astype(F32)

            @pl.when(first)
            def _():
                pad[q, 0, 8:8 + S, :] = tl[0, q, 8:8 + S, :]
                pad[q, 0, 8 + S:8 + H, :] = lh[p, 0, q, 0:2 * S].astype(F32)

            @pl.when(jnp.logical_not(last))
            def _():
                pad[q, J + 1, 8:8 + H, :] = rh[p, 0, q].astype(F32)

            @pl.when(last)
            def _():
                pad[q, J + 1, 8:8 + 2 * S, :] = rh[p, 0, q, S:H].astype(F32)
                pad[q, J + 1, 8 + 2 * S:8 + H, :] = dl[0, q, 8:8 + S, :]
            top = product(one_hot(spread_a & (lane < S)), ap[p, 0, q], 1, 0)
            low = product(one_hot(spread_b & (lane >= 16)), bm[p, 0, q], 1, 0)
            for j in range(J + 2):
                pad[q, j, 7:8, :] = top[j:j + 1]
                pad[q, j, 8 + H:9 + H, :] = low[j:j + 1]
        for a in range(3):
            for b in range(3):
                for q in range(G):
                    for j in range(J):
                        m = (q * J + j) * H
                        out[3 * a + b, m:m + H, :] = pad[q, j + a, 7 + b:7 + b + H, :].astype(BF16)

    def backward_taps(p, src, out):
        fill_columns(1, src)
        for q in range(G):
            @pl.when(jnp.logical_not(first))
            def _():
                pad[q, 0, 8:8 + H, :] = lh[p, 1, q].astype(F32)

            @pl.when(first)
            def _():
                pad[q, 0, :, :] = jnp.zeros((H + 16, C), F32)

            @pl.when(jnp.logical_not(last))
            def _():
                pad[q, J + 1, 8:8 + H, :] = rh[p, 1, q].astype(F32)

            @pl.when(last)
            def _():
                pad[q, J + 1, :, :] = jnp.zeros((H + 16, C), F32)
            for j in range(J + 2):
                pad[q, j, 7:8, :] = jnp.zeros((1, C), F32)
                pad[q, j, 8 + H:9 + H, :] = jnp.zeros((1, C), F32)
        for a in range(3):
            for b in range(3):
                for q in range(G):
                    for j in range(J):
                        m = (q * J + j) * H
                        out[3 * a + b, m:m + H, :] = pad[q, j - a + 2, 9 - b:9 - b + H, :]
        for q in range(G):
            top = product(one_hot(spread_a), ap[p, 1, q], 1, 0)
            low = product(one_hot(spread_b), bm[p, 1, q], 1, 0)
            for b in range(3):
                for j in range(J):
                    m = (q * J + j) * H
                    out[b, m:m + 1, :] += top[j + 2 - b:j + 3 - b]
                    out[6 + b, m + H - 1:m + H, :] += low[j + 2 - b:j + 3 - b]

        @pl.when(last)
        def _():
            for q in range(G):
                m = (q * J + J - 1) * H
                pad[q, J + 1, 8:8 + H, :] = rh[p, 1, q].astype(F32)
                for e in range(3):
                    out[e, m:m + 2 * S, :] += pad[q, J + 1, 8 + S + 1 - e:8 + H + 1 - e, :]
                    out[3 * e + 2, m + 2 * S:m + H, :] += dl[1, q, 9 - e:9 - e + S, :]

        @pl.when(first)
        def _():
            for q in range(G):
                m = q * J * H
                pad[q, 0, 8:8 + H, :] = lh[p, 1, q].astype(F32)
                for e in range(3):
                    out[3 * e, m:m + S, :] += tl[1, q, 9 - e:9 - e + S, :]
                    pass
                for e in range(3):
                    out[6 + e, m + S:m + H, :] += pad[q, 0, 9 - e:9 - e + 2 * S, :]

    def apply(taps, k, dim):
        total = product(taps[0].astype(BF16), k[0, 0], 1, dim)
        for n in range(1, 9):
            total = total + product(taps[n].astype(BF16), k[n // 3, n % 3], 1, dim)
        return total

    def flat(src, u):
        return jnp.concatenate([src[u, q, j] for q in range(G) for j in range(J)], axis=0)

    per = C // 16

    def weight_terms(taps, cot, base):
        for n in range(9):
            term = product(taps[n], cot, 0, 0) * scale
            acc[base + n * per:base + (n + 1) * per] = term.reshape(per, 16, C)

    barrier = pltpu.get_barrier_semaphore()

    @pl.loop(0, n_f)
    def _(df):
        @pl.loop(0, n_t)
        def _(dt):
            @pl.when(jnp.logical_or(df != f, dt != t))
            def _():
                pl.semaphore_signal(barrier, inc=1, device_id=where_to(dt, df), device_id_type=MESH)
    stage_rows(0, x)
    tl[...] = jnp.zeros_like(tl)
    dl[...] = jnp.zeros_like(dl)
    pad[...] = jnp.zeros_like(pad)
    blocks = acc.shape[0]
    if blocks > 18 * per:
        acc[18 * per:blocks] = jnp.zeros((blocks - 18 * per, 16, C), F32)
    pl.semaphore_wait(barrier, n_t * n_f - 1)

    start(0, x)
    await_arrivals(0, x)
    forward_taps(0, x, xf1)
    pre_one = apply(xf1, k1, 0)
    value, slope = gelu_parts(pre_one)
    backward_taps(0, x, xb)
    pre_grad = (apply(xb, k2, 1) * slope).astype(BF16)
    value = value.astype(BF16)
    for q in range(G):
        for j in range(J):
            m = (q * J + j) * H
            y[0, q, j] = value[m:m + H]
            y[1, q, j] = pre_grad[m:m + H]
    stage_rows(1, y)
    start(1, y)
    weight_terms(xf1, pre_grad, 0)
    await_arrivals(1, y)
    forward_taps(1, y, xf2)
    weight_terms(xf2, flat(x, 1), 9 * per)

    steps = []
    size = 1
    tile_bits, face_bits = [], []
    while size < n_t:
        tile_bits.append(size)
        size *= 2
    size = 1
    while size < n_f:
        face_bits.append(size)
        size *= 2
    order = [("tile", s) for s in tile_bits[:1]] + [("face", s) for s in face_bits] + [("tile", s) for s in tile_bits[1:]]

    def partner(axis, s):
        me = t if axis == "tile" else f
        bit = lax.rem(me // s, 2)
        other = me + (1 - 2 * bit) * s
        return bit, (where_to(other, f) if axis == "tile" else where_to(t, other))

    lo = 0
    length = blocks
    offset = 0
    for n, (axis, s) in enumerate(order):
        bit, dev = partner(axis, s)
        half = length // 2
        keep = lo + bit * half
        give = lo + (1 - bit) * half
        sbuf[pl.ds(give, half)] = acc[pl.ds(give, half)].astype(BF16)
        copy = remote(sbuf.at[pl.ds(give, half)], rbuf.at[offset:offset + half], w_s.at[n], w_r.at[n], dev)
        copy.start()
        if n == 0:
            out = apply(xf2, k2, 0).astype(BF16)
            for q in range(G):
                for j in range(J):
                    m = (q * J + j) * H
                    res_o[q, j] = out[m:m + H]
            backward_taps(1, y, xb)
            out = apply(xb, k1, 1).astype(BF16)
            for q in range(G):
                for j in range(J):
                    m = (q * J + j) * H
                    fg_o[q, j] = out[m:m + H]
        copy.wait()
        acc[pl.ds(keep, half)] += rbuf[offset:offset + half].astype(F32)
        steps.append((bit, dev, lo, keep, half))
        offset += half
        lo = keep
        length = half
    obuf[pl.ds(lo, length)] = acc[pl.ds(lo, length)].astype(BF16)
    for n, (bit, dev, before, keep, half) in reversed(list(enumerate(steps))):
        m = len(order) + n
        copy = remote(obuf.at[pl.ds(keep, half)], obuf.at[pl.ds(keep, half)], w_s.at[m], w_r.at[m], dev)
        copy.start()
        copy.wait()
    for n in range(9):
        w1_o[n] = obuf[n * per:(n + 1) * per].astype(F32).reshape(C, C)
        w2_o[n] = obuf[(9 + n) * per:(10 + n) * per].astype(F32).reshape(C, C)
    await_sends(0, x)
    await_sends(1, y)


def run(x, k1, k2, n_t, n_f):
    _, G, J, H, C = x.shape
    S = H // 3
    W = S + 16
    M = G * J * H
    ranks = n_t * n_f
    blocks = -(-(18 * (C // 16)) // ranks) * ranks
    scale = 1.0 / (S * 12.0 ** 0.5)
    bits = (n_t.bit_length() - 1) + (n_f.bit_length() - 1)
    dma = pltpu.SemaphoreType.DMA
    vmem = pl.BlockSpec(memory_space=pltpu.VMEM)
    return pl.pallas_call(
        functools.partial(body, n_t, n_f, scale),
        out_shape=(
            jax.ShapeDtypeStruct((G, J, H, C), BF16),
            jax.ShapeDtypeStruct((G, J, H, C), BF16),
            jax.ShapeDtypeStruct((9, C, C), F32),
            jax.ShapeDtypeStruct((9, C, C), F32),
        ),
        in_specs=[vmem] * 3,
        out_specs=[vmem] * 4,
        scratch_shapes=[
            pltpu.VMEM((2, G, J, H, C), BF16),
            pltpu.VMEM((2, 2, 2, G, J, C), F32),
            pltpu.VMEM((2, 2, G, H, C), BF16),
            pltpu.VMEM((2, 2, G, H, C), BF16),
            pltpu.VMEM((2, 2, G, W, C), BF16),
            pltpu.VMEM((2, 2, G, W, C), BF16),
            pltpu.VMEM((2, n_t, 2, G, J, C), F32),
            pltpu.VMEM((2, n_t, 2, G, J, C), F32),
            pltpu.VMEM((2, G, S + 16, C), F32),
            pltpu.VMEM((2, G, S + 16, C), F32),
            pltpu.VMEM((G, J + 2, H + 16, C), F32),
            pltpu.VMEM((9, M, C), F32),
            pltpu.VMEM((9, M, C), BF16),
            pltpu.VMEM((9, M, C), BF16),
            pltpu.VMEM((blocks, 16, C), F32),
            pltpu.VMEM((blocks, 16, C), BF16),
            pltpu.VMEM((blocks, 16, C), BF16),
            pltpu.VMEM((blocks, 16, C), BF16),
            dma((2, 6)), dma((2, 6)),
            dma((2, 2, n_t)), dma((2, 2)),
            dma((2, 2, n_t)), dma((2, 2)),
            dma((2, 2)), dma((2, 2, n_t)),
            dma((2, 2)), dma((2, 2, n_t)),
            dma((2 * bits,)), dma((2 * bits,)),
        ],
        compiler_params=pltpu.CompilerParams(
            collective_id=0, has_side_effects=True, vmem_limit_bytes=56 * 1024 * 1024),
    )(x, k1, k2)


def on_device(n_sub, n_t, n_f, fields, upstream, k1, k2):
    own = fields.shape[0]
    if n_sub > 1:
        fields = lax.all_gather(fields, "sub", axis=0, tiled=True)
        upstream = lax.all_gather(upstream, "sub", axis=0, tiled=True)
    x = jnp.stack([fields, upstream]).transpose(0, 2, 3, 4, 1)
    res, fgrad, w1, w2 = run(x, k1, k2, n_t, n_f)
    if n_sub > 1:
        at = lax.axis_index("sub") * own
        res = lax.dynamic_slice_in_dim(res, at, own, 3)
        fgrad = lax.dynamic_slice_in_dim(fgrad, at, own, 3)
        w1 = lax.dynamic_slice_in_dim(w1, at, own, 2)
        w2 = lax.dynamic_slice_in_dim(w2, at, own, 2)
    shape = (3, 3) + w1.shape[1:]
    return (res.transpose(3, 0, 1, 2), fgrad.transpose(3, 0, 1, 2), w1.reshape(shape), w2.reshape(shape))


def solution(mesh):
    placed = (P("sub", "face", "tile", "parts"), P("sub", "face", "tile", "parts"), P(), P())
    sizes = mesh.shape
    return jax.shard_map(
        functools.partial(on_device, sizes["sub"], sizes["tile"], sizes["face"]),
        mesh=mesh,
        in_specs=placed,
        out_specs=(
            P("sub", "face", "tile", "parts"),
            P("sub", "face", "tile", "parts"),
            P("parts", None, None, "sub"),
            P("parts", None, None, "sub"),
        ),
        check_vma=False,
    )
```

profile of v0, /device:TPU:0, one launch (start us, length us, event | category | flops | bytes accessed | tf_op | source)
XLA Modules:
  0.0 75.0 jit_solution(15010591081782272851)
XLA Ops:
  0.6 0.0 copy-start.1
  0.6 1.0 %copy.8 = bf16[96,2,2,96]{0,3,2,1:T(8,128)(2,1)S(1)} copy(bf16[96,2,2,96]{3,2,1,0:T(2,128)(2,1)} %param.4) | data formatting | bytes 147456 | tf_op args[0]
  1.7 0.0 copy-done.1
  1.7 0.1 copy.9
  1.8 0.7 maximum_bitcast_fusion.x
  2.5 67.4 %shard_map.75 = (bf16[2,2,96,96]{3,2,1,0:T(8,128)(2,1)}, bf16[2,2,96,96]{3,2,1,0:T(8,128)(2,1)}, f32[9,96,96]{2,1,0:T(8,128)}, f32[9,96,96]{2,1,0:T(8,128)}) custom-call(bf16[2,2,2,96,96]{4,3,2,1,0:T(8,128)(2,1)} %maximum_bitcast_fusion.x, bf16[3,3,96,96]{3,2,1,0:T(8,128)(2,1)} %k1.1, bf16[3,3,96,96]{3,2,1,0:T(8,128)(2,1)} %k2.1), custom_call_target="tpu_custom_call" | custom-call | tf_op jit(solution)/shard_map/pallas_call | solution.py:453
  69.9 0.0 copy-start.2
  69.9 1.7 %copy.10 = bf16[96,2,2,96]{3,2,1,0:T(2,128)(2,1)} copy(bf16[96,2,2,96]{0,3,2,1:T(8,128)(2,1)} %bitcast.13) | data formatting | bytes 147456
  71.6 0.0 copy-done.2
  71.6 0.8 %copy.11 = bf16[96,2,2,96]{3,2,1,0:T(2,128)(2,1)} copy(bf16[96,2,2,96]{0,3,2,1:T(8,128)(2,1)S(1)} %bitcast.12) | data formatting | bytes 147456
  72.4 0.0 copy-start
  72.4 1.9 %copy.14 = f32[3,3,96,96]{3,2,1,0:T(8,128)} copy(f32[3,3,96,96]{3,2,1,0:T(8,128)} %bitcast.9) | data formatting | bytes 663552
  74.2 0.0 copy-done
  74.2 0.8 %copy.15 = f32[3,3,96,96]{3,2,1,0:T(8,128)} copy(f32[3,3,96,96]{3,2,1,0:T(8,128)S(1)} %bitcast.8) | data formatting | bytes 663552
Async XLA Ops:
  0.6 1.1 %copy-start.1 = (bf16[96,2,2,96]{3,2,1,0:T(2,128)(2,1)S(1)}, bf16[96,2,2,96]{3,2,1,0:T(2,128)(2,1)}, u32[]{:S(2)}) copy-start(bf16[96,2,2,96]{3,2,1,0:T(2,128)(2,1)} %param.5) | copy-start | bytes 221188
  69.9 1.7 %copy-start.2 = (bf16[2,2,96,96]{3,2,1,0:T(8,128)(2,1)S(1)}, bf16[2,2,96,96]{3,2,1,0:T(8,128)(2,1)}, u32[]{:S(2)}) copy-start(bf16[2,2,96,96]{3,2,1,0:T(8,128)(2,1)} %get-tuple-element.9) | copy-start | bytes 221188
  72.4 1.9 %copy-start = (f32[9,96,96]{2,1,0:T(8,128)S(1)}, f32[9,96,96]{2,1,0:T(8,128)}, u32[]{:S(2)}) copy-start(f32[9,96,96]{2,1,0:T(8,128)} %get-tuple-element.11) | copy-start | bytes 995332
where the time goes:
time: 75.2 us; the launch traced here: 75 us
  Pallas kernels  67.4 us (90%)
  local copies, waits for them, and re-layouts  6.22 us (8%)
    pallas_call x1, Pallas kernels, run(): pl.pallas_call(functools.partial(body, n_t, n_f, scale), out_shape=(jax.S...  67.4 us
    unnamed x12, local copies, waits for them, and re-layouts  6.22 us

commit v1 on v0

v1 whole, which is shorter than its diff:
```python
import functools

import jax
import jax.numpy as jnp
from jax import lax
from jax.experimental import pallas as pl
from jax.experimental.pallas import tpu as pltpu
from jax.sharding import PartitionSpec as P

MESH = pl.DeviceIdType.MESH
F32 = jnp.float32
BF16 = jnp.bfloat16


def gelu_parts(v):
    root = 0.7978845608028654
    cube = 0.044715 * (v * v * v)
    th = jnp.tanh(root * (v + cube))
    value = v * (0.5 * (1.0 + th))
    slope = 0.5 * (1.0 + th) + 0.5 * v * (1.0 - th * th) * root * (1.0 + 0.134145 * (v * v))
    return value, slope


def product(a, b, da, db):
    return lax.dot_general(a, b, (((da,), (db,)), ((), ())), preferred_element_type=F32)


def body(n_t, n_f, scale, groups, x, k1, k2, res_o, fg_o, w1_o, w2_o,
         y, rows, lh, rh, ap, bm, aps, tr, dr, tl, dl, al, pad, xb, xf1, xf2,
         acc, sbuf, rlow, rfull, obuf,
         col_s, col_r, a_s, a_r, b_s, b_r, t_s, t_r, d_s, d_r, w_s, w_r):
    _, G, J, H, C = x.shape
    S = H // 3
    E = J + 2
    t = lax.axis_index("tile")
    f = lax.axis_index("face")
    fn = lax.rem(f + 1, n_f)
    fp = lax.rem(f + n_f - 1, n_f)
    first = t == 0
    last = t == n_t - 1
    inner_left = jnp.logical_not(first)
    inner_right = jnp.logical_not(last)

    def where_to(tile, face):
        return {"tile": tile, "face": face}

    def remote(src, dst, s, r, dev):
        return pltpu.make_async_remote_copy(
            src_ref=src, dst_ref=dst, send_sem=s, recv_sem=r, device_id=dev, device_id_type=MESH)

    def copies(p, src):
        c0, cl = src.at[:, 0], src.at[:, J - 1]
        right = lambda: remote(cl, lh.at[p], col_s.at[p, 0], col_r.at[p, 0], where_to(jnp.minimum(t + 1, n_t - 1), f))
        left = lambda: remote(c0, rh.at[p], col_s.at[p, 1], col_r.at[p, 1], where_to(jnp.maximum(t - 1, 0), f))
        seam = []
        if G > 1:
            seam.append((first, lambda: remote(src.at[1:G, 0], rh.at[p, 0:G - 1], col_s.at[p, 2], col_r.at[p, 2], where_to(n_t - 1, f))))
            seam.append((last, lambda: remote(src.at[0:G - 1, J - 1], lh.at[p, 1:G], col_s.at[p, 3], col_r.at[p, 3], where_to(0, f))))
        seam.append((first, lambda: remote(src.at[0:1, 0], rh.at[p, G - 1:G], col_s.at[p, 4], col_r.at[p, 4], where_to(n_t - 1, fp))))
        seam.append((last, lambda: remote(src.at[G - 1:G, J - 1], lh.at[p, 0:1], col_s.at[p, 5], col_r.at[p, 5], where_to(0, fn))))
        a_own = lambda d: remote(aps.at[p, d, 1:G], ap.at[p, 0:G - 1], a_s.at[p, 0, d], a_r.at[p, 0], where_to(d, f))
        a_oth = lambda d: remote(aps.at[p, d, 0:1], ap.at[p, G - 1:G], a_s.at[p, 1, d], a_r.at[p, 1], where_to(d, fp))
        b_own = lambda d: remote(aps.at[p, d, 0:G - 1], bm.at[p, 1:G], b_s.at[p, 0, d], b_r.at[p, 0], where_to(d, f))
        b_oth = lambda d: remote(aps.at[p, d, G - 1:G], bm.at[p, 0:1], b_s.at[p, 1, d], b_r.at[p, 1], where_to(d, fn))
        t_own = lambda d: remote(rows.at[p, 0, 0:G - 1], tr.at[p, d, 1:G], t_s.at[p, 0], t_r.at[p, 0, d], where_to(0, f))
        t_oth = lambda d: remote(rows.at[p, 0, G - 1:G], tr.at[p, d, 0:1], t_s.at[p, 1], t_r.at[p, 1, d], where_to(0, fn))
        d_own = lambda d: remote(rows.at[p, 1, 1:G], dr.at[p, d, 0:G - 1], d_s.at[p, 0], d_r.at[p, 0, d], where_to(n_t - 1, f))
        d_oth = lambda d: remote(rows.at[p, 1, 0:1], dr.at[p, d, G - 1:G], d_s.at[p, 1], d_r.at[p, 1, d], where_to(n_t - 1, fp))
        return right, left, seam, a_own, a_oth, b_own, b_oth, t_own, t_oth, d_own, d_oth

    def stage(p, src):
        for q in range(G):
            for j in range(J):
                rows[p, 0, q, j:j + 1, :] = src[q, j, 0:16].astype(F32)[0:1]
                rows[p, 1, q, j:j + 1, :] = src[q, j, H - 16:H].astype(F32)[15:16]

        @pl.when(first)
        def _():
            more = 16 * (p % 2)
            for q in range(G):
                al[p % 2, q, 16:16 + S + more, :] = src[q, 0, 0:S + more].astype(F32)
            for d in range(n_t):
                aps[p, d] = al[p % 2, :, 15 + d * J:15 + d * J + E, :]

        @pl.when(last)
        def _():
            more = 16 * (p % 2)
            for q in range(G):
                al[p % 2, q, 16 - more:16 + S, :] = src[q, J - 1, 2 * S - more:H].astype(F32)
            for d in range(n_t):
                aps[p, d] = al[p % 2, :, 15 + d * J:15 + d * J + E, :]

    def start(p, src):
        right, left, seam, a_own, a_oth, b_own, b_oth, t_own, t_oth, d_own, d_oth = copies(p, src)
        t_oth(t).start()
        d_oth(t).start()
        if G > 1:
            @pl.when(inner_left)
            def _():
                t_own(t).start()

            @pl.when(inner_right)
            def _():
                d_own(t).start()
        for cond, make in seam:
            @pl.when(cond)
            def _(make=make):
                make().start()

        @pl.when(first)
        def _():
            @pl.loop(0, n_t)
            def _(d):
                a_oth(n_t - 1 - d).start()
            if G > 1:
                @pl.loop(1, n_t)
                def _(d):
                    a_own(n_t - d).start()
                ap[p, 0:G - 1] = aps[p, 0, 1:G]
                tr[p, 0, 1:G] = rows[p, 0, 0:G - 1]

        @pl.when(last)
        def _():
            @pl.loop(0, n_t)
            def _(d):
                b_oth(d).start()
            if G > 1:
                @pl.loop(0, n_t - 1)
                def _(d):
                    b_own(d).start()
                bm[p, 1:G] = aps[p, n_t - 1, 0:G - 1]
                dr[p, n_t - 1, 0:G - 1] = rows[p, 1, 1:G]

        @pl.when(inner_right)
        def _():
            right().start()

        @pl.when(inner_left)
        def _():
            left().start()

    def await_arrivals(p, src):
        right, left, seam, a_own, a_oth, b_own, b_oth, t_own, t_oth, d_own, d_oth = copies(p, src)

        @pl.when(inner_left)
        def _():
            right().wait_recv()
            if G > 1:
                a_own(0).wait_recv()

        @pl.when(inner_right)
        def _():
            left().wait_recv()
            if G > 1:
                b_own(0).wait_recv()

        for cond, make in seam:
            @pl.when(last if cond is first else first)
            def _(make=make):
                make().wait_recv()

        a_oth(0).wait_recv()
        b_oth(0).wait_recv()

        @pl.when(first)
        def _():
            if G > 1:
                @pl.loop(1, n_t)
                def _(d):
                    t_own(d).wait_recv()

            @pl.loop(0, n_t)
            def _(d):
                t_oth(d).wait_recv()
            for d in range(n_t):
                tl[p % 2, :, 8 + d * J:8 + (d + 1) * J, :] = tr[p, d]

        @pl.when(last)
        def _():
            if G > 1:
                @pl.loop(0, n_t - 1)
                def _(d):
                    d_own(d).wait_recv()

            @pl.loop(0, n_t)
            def _(d):
                d_oth(d).wait_recv()
            for d in range(n_t):
                dl[p % 2, :, 8 + d * J:8 + (d + 1) * J, :] = dr[p, d]

    def await_sends(p, src):
        right, left, seam, a_own, a_oth, b_own, b_oth, t_own, t_oth, d_own, d_oth = copies(p, src)

        @pl.when(inner_right)
        def _():
            right().wait_send()
            if G > 1:
                d_own(t).wait_send()

        @pl.when(inner_left)
        def _():
            left().wait_send()
            if G > 1:
                t_own(t).wait_send()

        for cond, make in seam:
            @pl.when(cond)
            def _(make=make):
                make().wait_send()
        t_oth(t).wait_send()
        d_oth(t).wait_send()

        @pl.when(first)
        def _():
            if G > 1:
                @pl.loop(1, n_t)
                def _(d):
                    a_own(d).wait_send()

            @pl.loop(0, n_t)
            def _(d):
                a_oth(d).wait_send()

        @pl.when(last)
        def _():
            if G > 1:
                @pl.loop(0, n_t - 1)
                def _(d):
                    b_own(d).wait_send()

            @pl.loop(0, n_t)
            def _(d):
                b_oth(d).wait_send()

    def fill_columns(src):
        for q in range(G):
            for j in range(J):
                pad[q, 1 + j, 8:8 + H, :] = src[q, j].astype(F32)

    def forward_taps(p, src, out):
        fill_columns(src)
        for q in range(G):
            @pl.when(inner_left)
            def _():
                pad[q, 0, 8:8 + H, :] = lh[p, q].astype(F32)

            @pl.when(first)
            def _():
                pad[q, 0, 8:8 + S, :] = tl[0, q, 8:8 + S, :]
                pad[q, 0, 8 + S:8 + H, :] = lh[p, q, 0:2 * S].astype(F32)

            @pl.when(inner_right)
            def _():
                pad[q, J + 1, 8:8 + H, :] = rh[p, q].astype(F32)

            @pl.when(last)
            def _():
                pad[q, J + 1, 8:8 + 2 * S, :] = rh[p, q, S:H].astype(F32)
                pad[q, J + 1, 8 + 2 * S:8 + H, :] = dl[0, q, 8:8 + S, :]
            for j in range(E):
                pad[q, j, 7:8, :] = ap[p, q, j:j + 1]
                pad[q, j, 8 + H:9 + H, :] = bm[p, q, j:j + 1]
        for a in range(3):
            for b in range(3):
                for q in range(G):
                    for j in range(J):
                        m = (q * J + j) * H
                        out[3 * a + b, m:m + H, :] = pad[q, j + a, 7 + b:7 + b + H, :].astype(BF16)

    def backward_taps(p, src, out):
        fill_columns(src)
        for q in range(G):
            @pl.when(inner_left)
            def _():
                pad[q, 0, 8:8 + H, :] = lh[p, q].astype(F32)

            @pl.when(first)
            def _():
                pad[q, 0, :, :] = jnp.zeros((H + 16, C), F32)

            @pl.when(inner_right)
            def _():
                pad[q, J + 1, 8:8 + H, :] = rh[p, q].astype(F32)

            @pl.when(last)
            def _():
                pad[q, J + 1, :, :] = jnp.zeros((H + 16, C), F32)
            for j in range(E):
                pad[q, j, 7:8, :] = jnp.zeros((1, C), F32)
                pad[q, j, 8 + H:9 + H, :] = jnp.zeros((1, C), F32)
        for a in range(3):
            for b in range(3):
                for q in range(G):
                    for j in range(J):
                        m = (q * J + j) * H
                        out[3 * a + b, m:m + H, :] = pad[q, j - a + 2, 9 - b:9 - b + H, :]
        for q in range(G):
            top = ap[p, q]
            low = bm[p, q]
            for b in range(3):
                for j in range(J):
                    m = (q * J + j) * H
                    out[b, m:m + 1, :] += top[j + 2 - b:j + 3 - b]
                    out[6 + b, m + H - 1:m + H, :] += low[j + 2 - b:j + 3 - b]

        @pl.when(last)
        def _():
            for q in range(G):
                m = (q * J + J - 1) * H
                pad[q, J + 1, 8:8 + H, :] = rh[p, q].astype(F32)
                for e in range(3):
                    out[e, m:m + 2 * S, :] += pad[q, J + 1, 8 + S + 1 - e:8 + H + 1 - e, :]
                    out[3 * e + 2, m + 2 * S:m + H, :] += dl[1, q, 9 - e:9 - e + S, :]

        @pl.when(first)
        def _():
            for q in range(G):
                m = q * J * H
                pad[q, 0, 8:8 + H, :] = lh[p, q].astype(F32)
                for e in range(3):
                    out[3 * e, m:m + S, :] += tl[1, q, 9 - e:9 - e + S, :]
                    out[6 + e, m + S:m + H, :] += pad[q, 0, 9 - e:9 - e + 2 * S, :]

    def apply(taps, k, dim):
        total = product(taps[0].astype(BF16), k[0, 0], 1, dim)
        for n in range(1, 9):
            total = total + product(taps[n].astype(BF16), k[n // 3, n % 3], 1, dim)
        return total

    def flat(src):
        return jnp.concatenate([src[q, j] for q in range(G) for j in range(J)], axis=0)

    def unflat(value, dst):
        for q in range(G):
            for j in range(J):
                m = (q * J + j) * H
                dst[q, j] = value[m:m + H]

    per = C // 16
    blocks = acc.shape[1]

    def weight_terms(taps, cot, w):
        for n in range(9):
            term = product(taps[n], cot, 0, 0) * scale
            acc[w, n * per:(n + 1) * per] = term.reshape(per, 16, C)

    class Sum:
        def __init__(self, w):
            self.w, self.lo, self.length, self.done = w, 0, blocks, []
            self.used = [0, 0]
            self.sem = 0

        def members(self, bits):
            mine, place = [], 0
            for axis, s in bits:
                mine.append(lax.rem((t if axis == "tile" else f) // s, 2))
            found = []
            for k in range(1, 2 ** len(bits)):
                tile, face, digit = t, f, 0
                for pos, (axis, s) in enumerate(bits):
                    bit = mine[pos]
                    if (k >> pos) & 1:
                        if axis == "tile":
                            tile = tile + (1 - 2 * bit) * s
                        else:
                            face = face + (1 - 2 * bit) * s
                        bit = 1 - bit
                    digit = digit + bit * (1 << pos)
                found.append((digit, where_to(tile, face)))
            own = 0
            for pos, bit in enumerate(mine):
                own = own + bit * (1 << pos)
            return own, found

        def begin(self, n):
            bits, full = groups[n]
            own, found = self.members(bits)
            part = self.length // (len(found) + 1)
            w = self.w
            inbox = rfull if full else rlow
            self.flying = []
            for digit, dev in found:
                give = self.lo + digit * part
                at = self.used[full]
                self.used[full] += part
                if full:
                    out = acc.at[w, pl.ds(give, part)]
                else:
                    sbuf[w, pl.ds(give, part)] = acc[w, pl.ds(give, part)].astype(BF16)
                    out = sbuf.at[w, pl.ds(give, part)]
                copy = remote(out, inbox.at[w, at:at + part], w_s.at[w, self.sem], w_r.at[w, self.sem], dev)
                self.sem += 1
                copy.start()
                self.flying.append((copy, inbox, at))
            keep = self.lo + own * part
            self.done.append((keep, part, found))
            self.lo, self.length = keep, part

        def end(self):
            total = acc[self.w, pl.ds(self.lo, self.length)]
            for copy, inbox, at in self.flying:
                copy.wait()
                total = total + inbox[self.w, at:at + self.length].astype(F32)
            acc[self.w, pl.ds(self.lo, self.length)] = total

        def round(self):
            obuf[self.w, pl.ds(self.lo, self.length)] = acc[self.w, pl.ds(self.lo, self.length)].astype(BF16)

        def give(self, n):
            keep, part, found = self.done[n]
            self.flying = []
            for digit, dev in found:
                copy = remote(obuf.at[self.w, pl.ds(keep, part)], obuf.at[self.w, pl.ds(keep, part)],
                              w_s.at[self.w, self.sem], w_r.at[self.w, self.sem], dev)
                self.sem += 1
                copy.start()
                self.flying.append(copy)

        def given(self):
            for copy in self.flying:
                copy.wait()

    barrier = pltpu.get_barrier_semaphore()

    @pl.loop(0, n_f)
    def _(df):
        @pl.loop(0, n_t)
        def _(dt):
            @pl.when(jnp.logical_or(df != f, dt != t))
            def _():
                pl.semaphore_signal(barrier, inc=1, device_id=where_to(dt, df), device_id_type=MESH)
    fields, upstream, hidden, pre_grad = x.at[0], x.at[1], y.at[0], y.at[1]
    al[...] = jnp.zeros_like(al)
    tl[...] = jnp.zeros_like(tl)
    dl[...] = jnp.zeros_like(dl)
    stage(0, fields)
    stage(1, upstream)
    if blocks > 9 * per:
        for w in range(2):
            acc[w, 9 * per:blocks] = jnp.zeros((blocks - 9 * per, 16, C), F32)
    pl.semaphore_wait(barrier, n_t * n_f - 1)

    start(0, fields)
    start(1, upstream)
    await_arrivals(0, fields)
    forward_taps(0, fields, xf1)
    value, slope = gelu_parts(apply(xf1, k1, 0))
    unflat(value.astype(BF16), hidden)
    stage(2, hidden)
    start(2, hidden)
    await_arrivals(1, upstream)
    backward_taps(1, upstream, xb)
    cot = (apply(xb, k2, 1) * slope).astype(BF16)
    unflat(cot, pre_grad)
    stage(3, pre_grad)
    start(3, pre_grad)
    sums = [Sum(0), Sum(1)]
    weight_terms(xf1, cot, 0)
    sums[0].begin(0)
    await_arrivals(2, hidden)
    forward_taps(2, hidden, xf2)
    weight_terms(xf2, flat(upstream), 1)
    sums[1].begin(0)
    sums[0].end()
    if len(groups) > 1:
        sums[0].begin(1)
    unflat(apply(xf2, k2, 0).astype(BF16), res_o)
    sums[1].end()
    if len(groups) > 1:
        sums[1].begin(1)
    await_arrivals(3, pre_grad)
    backward_taps(3, pre_grad, xb)
    unflat(apply(xb, k1, 1).astype(BF16), fg_o)
    for n in range(1, len(groups)):
        for total in sums:
            total.end()
            if n + 1 < len(groups):
                total.begin(n + 1)
    for total in sums:
        total.round()
    for n in reversed(range(len(groups))):
        for total in sums:
            if n + 1 < len(groups):
                total.given()
            total.give(n)
    for total, out in zip(sums, (w1_o, w2_o)):
        total.given()
        for n in range(9):
            out[n] = obuf[total.w, n * per:(n + 1) * per].astype(F32).reshape(C, C)
    await_sends(0, fields)
    await_sends(1, upstream)
    await_sends(2, hidden)
    await_sends(3, pre_grad)


def plan(n_t, n_f):
    tile_bits = [1 << i for i in range(n_t.bit_length() - 1)]
    face_bits = [1 << i for i in range(n_f.bit_length() - 1)]
    groups = [([("tile", tile_bits[0])], 1)]
    middle = [("face", s) for s in face_bits] + [("tile", s) for s in tile_bits[1:2]]
    rest = [("tile", s) for s in tile_bits[2:]]
    while middle:
        groups.append((middle[:2], 0))
        middle = middle[2:]
    while rest:
        groups.append((rest[:2], 1))
        rest = rest[2:]
    return groups


def run(x, k1, k2, n_t, n_f):
    _, G, J, H, C = x.shape
    S = H // 3
    E = J + 2
    M = G * J * H
    ranks = n_t * n_f
    blocks = -(-(9 * (C // 16)) // ranks) * ranks
    scale = 1.0 / (S * 12.0 ** 0.5)
    groups = plan(n_t, n_f)
    length, room, flights = blocks, [1, 1], 0
    for bits, full in groups:
        others = 2 ** len(bits) - 1
        length //= others + 1
        room[full] += length * others
        flights += others
    dma = pltpu.SemaphoreType.DMA
    vmem = pl.BlockSpec(memory_space=pltpu.VMEM)
    return pl.pallas_call(
        functools.partial(body, n_t, n_f, scale, groups),
        out_shape=(
            jax.ShapeDtypeStruct((G, J, H, C), BF16),
            jax.ShapeDtypeStruct((G, J, H, C), BF16),
            jax.ShapeDtypeStruct((9, C, C), F32),
            jax.ShapeDtypeStruct((9, C, C), F32),
        ),
        in_specs=[vmem] * 3,
        out_specs=[vmem] * 4,
        scratch_shapes=[
            pltpu.VMEM((2, G, J, H, C), BF16),
            pltpu.VMEM((4, 2, G, J, C), F32),
            pltpu.VMEM((4, G, H, C), BF16),
            pltpu.VMEM((4, G, H, C), BF16),
            pltpu.VMEM((4, G, E, C), F32),
            pltpu.VMEM((4, G, E, C), F32),
            pltpu.VMEM((4, n_t, G, E, C), F32),
            pltpu.VMEM((4, n_t, G, J, C), F32),
            pltpu.VMEM((4, n_t, G, J, C), F32),
            pltpu.VMEM((2, G, S + 16, C), F32),
            pltpu.VMEM((2, G, S + 16, C), F32),
            pltpu.VMEM((2, G, S + 32, C), F32),
            pltpu.VMEM((G, J + 2, H + 16, C), F32),
            pltpu.VMEM((9, M, C), F32),
            pltpu.VMEM((9, M, C), BF16),
            pltpu.VMEM((9, M, C), BF16),
            pltpu.VMEM((2, blocks, 16, C), F32),
            pltpu.VMEM((2, blocks, 16, C), BF16),
            pltpu.VMEM((2, room[0], 16, C), BF16),
            pltpu.VMEM((2, room[1], 16, C), F32),
            pltpu.VMEM((2, blocks, 16, C), BF16),
            dma((4, 6)), dma((4, 6)),
            dma((4, 2, n_t)), dma((4, 2)),
            dma((4, 2, n_t)), dma((4, 2)),
            dma((4, 2)), dma((4, 2, n_t)),
            dma((4, 2)), dma((4, 2, n_t)),
            dma((2, 2 * flights)), dma((2, 2 * flights)),
        ],
        compiler_params=pltpu.CompilerParams(
            collective_id=0, has_side_effects=True, vmem_limit_bytes=56 * 1024 * 1024),
    )(x, k1, k2)


def on_device(n_sub, n_t, n_f, fields, upstream, k1, k2):
    own = fields.shape[0]
    if n_sub > 1:
        fields = lax.all_gather(fields, "sub", axis=0, tiled=True)
        upstream = lax.all_gather(upstream, "sub", axis=0, tiled=True)
    x = jnp.stack([fields, upstream]).transpose(0, 2, 3, 4, 1)
    res, fgrad, w1, w2 = run(x, k1, k2, n_t, n_f)
    if n_sub > 1:
        at = lax.axis_index("sub") * own
        res = lax.dynamic_slice_in_dim(res, at, own, 3)
        fgrad = lax.dynamic_slice_in_dim(fgrad, at, own, 3)
        w1 = lax.dynamic_slice_in_dim(w1, at, own, 2)
        w2 = lax.dynamic_slice_in_dim(w2, at, own, 2)
    shape = (3, 3) + w1.shape[1:]
    return (res.transpose(3, 0, 1, 2), fgrad.transpose(3, 0, 1, 2), w1.reshape(shape), w2.reshape(shape))


def solution(mesh):
    placed = (P("sub", "face", "tile", "parts"), P("sub", "face", "tile", "parts"), P(), P())
    sizes = mesh.shape
    return jax.shard_map(
        functools.partial(on_device, sizes["sub"], sizes["tile"], sizes["face"]),
        mesh=mesh,
        in_specs=placed,
        out_specs=(
            P("sub", "face", "tile", "parts"),
            P("sub", "face", "tile", "parts"),
            P("parts", None, None, "sub"),
            P("parts", None, None, "sub"),
        ),
        check_vma=False,
    )
```

time: 75.2 us -> 52.8 us (0.70)
  Pallas kernels: 67.4 us -> 45 us
    pallas_call x1, Pallas kernels: 67.4 us -> 45 us  [run(): pl.pallas_call(functools.partial(body, n_t, n_f, scale, groups), out_shap...]
where the time goes in v1:
time: 52.8 us; the launch traced here: 52.6 us
  Pallas kernels  45 us (85%)
  local copies, waits for them, and re-layouts  6.22 us (12%)
  other arithmetic  0.72 us (1%)
  between operations  0.67 us (1%)
    pallas_call x1, Pallas kernels, run(): pl.pallas_call(functools.partial(body, n_t, n_f, scale, groups), out_shap...  45 us
    unnamed x12, local copies, waits for them, and re-layouts  6.22 us

profile of v1, /device:TPU:0, one launch (start us, length us, event | category | flops | bytes accessed | tf_op | source)
XLA Modules:
  0.0 52.6 jit_solution(6289634762087010058)
XLA Ops:
  0.6 0.0 copy-start.1
  0.6 1.0 %copy.8 = bf16[96,2,2,96]{0,3,2,1:T(8,128)(2,1)S(1)} copy(bf16[96,2,2,96]{3,2,1,0:T(2,128)(2,1)} %param.4) | data formatting | bytes 147456 | tf_op args[0]
  1.7 0.0 copy-done.1
  1.7 0.1 copy.9
  1.8 0.7 %maximum_bitcast_fusion.x = bf16[2,2,2,96,96]{4,3,2,1,0:T(8,128)(2,1)} fusion(bf16[1,96,2,2,96]{1,4,3,2,0:T(8,128)(2,1)S(1)} %bitcast.11, bf16[1,96,2,2,96]{1,4,3,2,0:T(8,128)(2,1)S(1)} %bitcast.10), kind=kLoop, calls=%fused_computation | loop fusion | flops 73728 | bytes 294912 | tf_op jit(solution)/shard_map/transpose | solution.py:577
  2.5 45.0 %shard_map.75 = (bf16[2,2,96,96]{3,2,1,0:T(8,128)(2,1)}, bf16[2,2,96,96]{3,2,1,0:T(8,128)(2,1)}, f32[9,96,96]{2,1,0:T(8,128)}, f32[9,96,96]{2,1,0:T(8,128)}) custom-call(bf16[2,2,2,96,96]{4,3,2,1,0:T(8,128)(2,1)} %maximum_bitcast_fusion.x, bf16[3,3,96,96]{3,2,1,0:T(8,128)(2,1)} %k1.1, bf16[3,3,96,96]{3,2,1,0:T(8,128)(2,1)} %k2.1), custom_call_target="tpu_custom_call" | custom-call | tf_op jit(solution)/shard_map/pallas_call | solution.py:528
  47.5 0.0 copy-start.2
  47.6 1.7 %copy.10 = bf16[96,2,2,96]{3,2,1,0:T(2,128)(2,1)} copy(bf16[96,2,2,96]{0,3,2,1:T(8,128)(2,1)} %bitcast.13) | data formatting | bytes 147456
  49.2 0.0 copy-done.2
  49.2 0.8 %copy.11 = bf16[96,2,2,96]{3,2,1,0:T(2,128)(2,1)} copy(bf16[96,2,2,96]{0,3,2,1:T(8,128)(2,1)S(1)} %bitcast.12) | data formatting | bytes 147456
  50.0 0.0 copy-start
  50.0 1.9 %copy.14 = f32[3,3,96,96]{3,2,1,0:T(8,128)} copy(f32[3,3,96,96]{3,2,1,0:T(8,128)} %bitcast.9) | data formatting | bytes 663552
  51.9 0.0 copy-done
  51.9 0.8 %copy.15 = f32[3,3,96,96]{3,2,1,0:T(8,128)} copy(f32[3,3,96,96]{3,2,1,0:T(8,128)S(1)} %bitcast.8) | data formatting | bytes 663552
Async XLA Ops:
  0.6 1.1 %copy-start.1 = (bf16[96,2,2,96]{3,2,1,0:T(2,128)(2,1)S(1)}, bf16[96,2,2,96]{3,2,1,0:T(2,128)(2,1)}, u32[]{:S(2)}) copy-start(bf16[96,2,2,96]{3,2,1,0:T(2,128)(2,1)} %param.5) | copy-start | bytes 221188
  47.5 1.7 %copy-start.2 = (bf16[2,2,96,96]{3,2,1,0:T(8,128)(2,1)S(1)}, bf16[2,2,96,96]{3,2,1,0:T(8,128)(2,1)}, u32[]{:S(2)}) copy-start(bf16[2,2,96,96]{3,2,1,0:T(8,128)(2,1)} %get-tuple-element.9) | copy-start | bytes 221188
  50.0 1.9 %copy-start = (f32[9,96,96]{2,1,0:T(8,128)S(1)}, f32[9,96,96]{2,1,0:T(8,128)}, u32[]{:S(2)}) copy-start(f32[9,96,96]{2,1,0:T(8,128)} %get-tuple-element.11) | copy-start | bytes 995332

commit v2 on v1

--- a/solution.py
+++ b/solution.py
@@ -25,10 +25,10 @@
     return lax.dot_general(a, b, (((da,), (db,)), ((), ())), preferred_element_type=F32)
 
 
-def body(n_t, n_f, scale, groups, x, k1, k2, res_o, fg_o, w1_o, w2_o,
-         y, rows, lh, rh, ap, bm, aps, tr, dr, tl, dl, al, pad, xb, xf1, xf2,
+def body(n_t, n_f, scale, groups, fields_h, upstream_h, k1_h, k2_h, res_o, fg_o, w1_o, w2_o,
+         x, k1, k2, y, rows, lh, rh, ap, bm, aps, tr, dr, tl, dl, al, pad, xb, xf1, xf2,
          acc, sbuf, rlow, rfull, obuf,
-         col_s, col_r, a_s, a_r, b_s, b_r, t_s, t_r, d_s, d_r, w_s, w_r):
+         col_s, col_r, a_s, a_r, b_s, b_r, t_s, t_r, d_s, d_r, w_s, w_r, in_s):
     _, G, J, H, C = x.shape
     S = H // 3
     E = J + 2
@@ -429,10 +429,16 @@
             @pl.when(jnp.logical_or(df != f, dt != t))
             def _():
                 pl.semaphore_signal(barrier, inc=1, device_id=where_to(dt, df), device_id_type=MESH)
+    loads = [pltpu.make_async_copy(src, dst, in_s.at[n]) for n, (src, dst) in enumerate(
+        ((fields_h, x.at[0]), (upstream_h, x.at[1]), (k1_h, k1), (k2_h, k2)))]
+    for load in loads:
+        load.start()
     fields, upstream, hidden, pre_grad = x.at[0], x.at[1], y.at[0], y.at[1]
     al[...] = jnp.zeros_like(al)
     tl[...] = jnp.zeros_like(tl)
     dl[...] = jnp.zeros_like(dl)
+    loads[0].wait()
+    loads[1].wait()
     stage(0, fields)
     stage(1, upstream)
     if blocks > 9 * per:
@@ -442,6 +448,8 @@
 
     start(0, fields)
     start(1, upstream)
+    loads[2].wait()
+    loads[3].wait()
     await_arrivals(0, fields)
     forward_taps(0, fields, xf1)
     value, slope = gelu_parts(apply(xf1, k1, 0))
@@ -486,7 +494,7 @@
     for total, out in zip(sums, (w1_o, w2_o)):
         total.given()
         for n in range(9):
-            out[n] = obuf[total.w, n * per:(n + 1) * per].astype(F32).reshape(C, C)
+            out[n] = obuf[total.w, n * per:(n + 1) * per].reshape(C, C)
     await_sends(0, fields)
     await_sends(1, upstream)
     await_sends(2, hidden)
@@ -503,13 +511,13 @@
         groups.append((middle[:2], 0))
         middle = middle[2:]
     while rest:
-        groups.append((rest[:2], 1))
+        groups.append((rest[:2], 0))
         rest = rest[2:]
     return groups
 
 
-def run(x, k1, k2, n_t, n_f):
-    _, G, J, H, C = x.shape
+def run(fields, upstream, k1, k2, n_t, n_f):
+    G, J, H, C = fields.shape
     S = H // 3
     E = J + 2
     M = G * J * H
@@ -530,12 +538,15 @@
         out_shape=(
             jax.ShapeDtypeStruct((G, J, H, C), BF16),
             jax.ShapeDtypeStruct((G, J, H, C), BF16),
-            jax.ShapeDtypeStruct((9, C, C), F32),
-            jax.ShapeDtypeStruct((9, C, C), F32),
+            jax.ShapeDtypeStruct((9, C, C), BF16),
+            jax.ShapeDtypeStruct((9, C, C), BF16),
         ),
-        in_specs=[vmem] * 3,
+        in_specs=[pl.BlockSpec(memory_space=pl.ANY)] * 2 + [pl.BlockSpec(memory_space=pltpu.HBM)] * 2,
         out_specs=[vmem] * 4,
         scratch_shapes=[
+            pltpu.VMEM((2, G, J, H, C), BF16),
+            pltpu.VMEM(k1.shape, BF16),
+            pltpu.VMEM(k2.shape, BF16),
             pltpu.VMEM((2, G, J, H, C), BF16),
             pltpu.VMEM((4, 2, G, J, C), F32),
             pltpu.VMEM((4, G, H, C), BF16),
@@ -562,11 +573,11 @@
             dma((4, 2, n_t)), dma((4, 2)),
             dma((4, 2)), dma((4, 2, n_t)),
             dma((4, 2)), dma((4, 2, n_t)),
-            dma((2, 2 * flights)), dma((2, 2 * flights)),
+            dma((2, 2 * flights)), dma((2, 2 * flights)), dma((4,)),
         ],
         compiler_params=pltpu.CompilerParams(
-            collective_id=0, has_side_effects=True, vmem_limit_bytes=56 * 1024 * 1024),
-    )(x, k1, k2)
+            collective_id=0, has_side_effects=True, vmem_limit_bytes=24 * 1024 * 1024),
+    )(fields, upstream, k1, k2)
 
 
 def on_device(n_sub, n_t, n_f, fields, upstream, k1, k2):
@@ -574,8 +585,8 @@
     if n_sub > 1:
         fields = lax.all_gather(fields, "sub", axis=0, tiled=True)
         upstream = lax.all_gather(upstream, "sub", axis=0, tiled=True)
-    x = jnp.stack([fields, upstream]).transpose(0, 2, 3, 4, 1)
-    res, fgrad, w1, w2 = run(x, k1, k2, n_t, n_f)
+    res, fgrad, w1, w2 = run(
+        fields.transpose(1, 2, 3, 0), upstream.transpose(1, 2, 3, 0), k1, k2, n_t, n_f)
     if n_sub > 1:
         at = lax.axis_index("sub") * own
         res = lax.dynamic_slice_in_dim(res, at, own, 3)
@@ -583,7 +594,7 @@
         w1 = lax.dynamic_slice_in_dim(w1, at, own, 2)
         w2 = lax.dynamic_slice_in_dim(w2, at, own, 2)
     shape = (3, 3) + w1.shape[1:]
-    return (res.transpose(3, 0, 1, 2), fgrad.transpose(3, 0, 1, 2), w1.reshape(shape), w2.reshape(shape))
+    return (res.transpose(3, 0, 1, 2), fgrad.transpose(3, 0, 1, 2), w1.astype(F32).reshape(shape), w2.astype(F32).reshape(shape))
 
 
 def solution(mesh):

time: 52.8 us -> 49.7 us (0.941)
  Pallas kernels: 45 us -> 42.7 us
  local copies, waits for them, and re-layouts: 6.22 us -> 4.51 us
  other arithmetic: 0.72 us -> 1.59 us
    pallas_call x1, Pallas kernels: 45 us -> 42.7 us  [run(): pl.pallas_call(functools.partial(body, n_t, n_f, scale, groups), out_shap...]
    unnamed x12 -> x8, local copies, waits for them, and re-layouts: 6.22 us -> 4.51 us
    reshape x0 -> x2, other arithmetic: none -> 1.59 us  [the longest x1 0.8 us: on_device(): w1.astype(F32).reshape(shape)]
    transpose x1 -> x0, other arithmetic: 0.72 us -> none  [on_device(): x = jnp.stack([fields, upstream]).transpose(0, 2, 3, 4, 1)]
where the time goes in v2:
time: 49.7 us; the launch traced here: 49.5 us
  Pallas kernels  42.7 us (86%)
  local copies, waits for them, and re-layouts  4.51 us (9%)
  other arithmetic  1.59 us (3%)
  between operations  0.67 us (1%)
    pallas_call x1, Pallas kernels, run(): pl.pallas_call(functools.partial(body, n_t, n_f, scale, groups), out_shap...  42.7 us
    unnamed x8, local copies, waits for them, and re-layouts  4.51 us

profile of v2, /device:TPU:0, one launch (start us, length us, event | category | flops | bytes accessed | tf_op | source)
XLA Modules:
  0.0 49.5 jit_solution(11308718301426442328)
XLA Ops:
  0.6 0.0 copy-start
  0.6 1.0 %copy.8 = bf16[96,2,2,96]{0,3,2,1:T(8,128)(2,1)S(1)} copy(bf16[96,2,2,96]{3,2,1,0:T(2,128)(2,1)} %param.4) | data formatting | bytes 147456 | tf_op args[0]
  1.7 1.0 %copy.9 = bf16[96,2,2,96]{0,3,2,1:T(8,128)(2,1)S(1)} copy(bf16[96,2,2,96]{3,2,1,0:T(2,128)(2,1)} %param.5) | data formatting | bytes 147456 | tf_op args[1]
  2.7 0.0 copy-done
  2.7 0.0 copy-start.1
  2.7 0.9 %copy-done.1 = bf16[3,3,96,96]{3,2,1,0:T(8,128)(2,1)S(1)} copy-done((bf16[3,3,96,96]{3,2,1,0:T(8,128)(2,1)S(1)}, bf16[3,3,96,96]{3,2,1,0:T(8,128)(2,1)}, u32[]{:S(2)}) %copy-start.1) | copy-done | bytes 165912
  3.7 42.7 %shard_map.75 = (bf16[2,2,96,96]{3,2,1,0:T(8,128)(2,1)S(1)}, bf16[2,2,96,96]{3,2,1,0:T(8,128)(2,1)S(1)}, bf16[9,96,96]{2,1,0:T(8,128)(2,1)S(1)}, bf16[9,96,96]{2,1,0:T(8,128)(2,1)S(1)}) custom-call(bf16[2,2,96,96]{3,2,1,0:T(8,128)(2,1)S(1)} %bitcast.8, bf16[2,2,96,96]{3,2,1,0:T(8,128)(2,1)S(1)} %bitcast.9, bf16[3,3,96,96]{3,2,1,0:T(8,128)(2,1)S(1)} %copy-done, ...), custom_call_target="tpu_custom_call" | custom-call | tf_op jit(solution)/shard_map/pallas_call | solution.py:536
  46.3 0.8 %copy.10 = bf16[96,2,2,96]{3,2,1,0:T(2,128)(2,1)} copy(bf16[96,2,2,96]{0,3,2,1:T(8,128)(2,1)S(1)} %bitcast.13) | data formatting | bytes 147456
  47.1 0.8 %copy.11 = bf16[96,2,2,96]{3,2,1,0:T(2,128)(2,1)} copy(bf16[96,2,2,96]{0,3,2,1:T(8,128)(2,1)S(1)} %bitcast.12) | data formatting | bytes 147456
  47.9 0.8 %convert.2 = f32[3,3,96,96]{3,2,1,0:T(8,128)} convert(bf16[3,3,96,96]{3,2,1,0:T(8,128)(2,1)S(1)} %bitcast.11) | non-fusion elementwise | flops 82944 | bytes 497664 | tf_op jit(solution)/shard_map/reshape | solution.py:597
  48.7 0.8 %convert.3 = f32[3,3,96,96]{3,2,1,0:T(8,128)} convert(bf16[3,3,96,96]{3,2,1,0:T(8,128)(2,1)S(1)} %bitcast.10) | non-fusion elementwise | flops 82944 | bytes 497664 | tf_op jit(solution)/shard_map/reshape | solution.py:597
Async XLA Ops:
  0.6 2.1 %copy-start = (bf16[3,3,96,96]{3,2,1,0:T(8,128)(2,1)S(1)}, bf16[3,3,96,96]{3,2,1,0:T(8,128)(2,1)}, u32[]{:S(2)}) copy-start(bf16[3,3,96,96]{3,2,1,0:T(8,128)(2,1)} %k1_h.1) | copy-start | bytes 497668
  2.7 0.9 %copy-start.1 = (bf16[3,3,96,96]{3,2,1,0:T(8,128)(2,1)S(1)}, bf16[3,3,96,96]{3,2,1,0:T(8,128)(2,1)}, u32[]{:S(2)}) copy-start(bf16[3,3,96,96]{3,2,1,0:T(8,128)(2,1)} %k2_h.1) | copy-start | bytes 497668

commit v3 on v2

--- a/solution.py
+++ b/solution.py
@@ -345,7 +345,8 @@
             acc[w, n * per:(n + 1) * per] = term.reshape(per, 16, C)
 
     class Sum:
-        def __init__(self, w):
+        def __init__(self, w, out):
+            self.out, self.at, self.over = out, 0, False
             self.w, self.lo, self.length, self.done = w, 0, blocks, []
             self.used = [0, 0]
             self.sem = 0
@@ -420,6 +421,26 @@
             for copy in self.flying:
                 copy.wait()
 
+        def advance(self):
+            at, count = self.at, len(groups)
+            self.at += 1
+            if at < count:
+                if at > 0:
+                    self.end()
+                self.begin(at)
+            elif at == count:
+                self.end()
+                self.round()
+                self.give(count - 1)
+            elif at < 2 * count:
+                self.given()
+                self.give(2 * count - 1 - at)
+            elif at == 2 * count:
+                self.given()
+                for n in range(9):
+                    self.out[n] = obuf[self.w, n * per:(n + 1) * per].reshape(C, C)
+                self.over = True
+
     barrier = pltpu.get_barrier_semaphore()
 
     @pl.loop(0, n_f)
@@ -462,39 +483,27 @@
     unflat(cot, pre_grad)
     stage(3, pre_grad)
     start(3, pre_grad)
-    sums = [Sum(0), Sum(1)]
+    one, two = Sum(0, w1_o), Sum(1, w2_o)
     weight_terms(xf1, cot, 0)
-    sums[0].begin(0)
+    one.advance()
+    one.advance()
     await_arrivals(2, hidden)
     forward_taps(2, hidden, xf2)
     weight_terms(xf2, flat(upstream), 1)
-    sums[1].begin(0)
-    sums[0].end()
-    if len(groups) > 1:
-        sums[0].begin(1)
+    two.advance()
+    one.advance()
+    two.advance()
     unflat(apply(xf2, k2, 0).astype(BF16), res_o)
-    sums[1].end()
-    if len(groups) > 1:
-        sums[1].begin(1)
+    one.advance()
+    two.advance()
     await_arrivals(3, pre_grad)
     backward_taps(3, pre_grad, xb)
+    one.advance()
+    two.advance()
     unflat(apply(xb, k1, 1).astype(BF16), fg_o)
-    for n in range(1, len(groups)):
-        for total in sums:
-            total.end()
-            if n + 1 < len(groups):
-                total.begin(n + 1)
-    for total in sums:
-        total.round()
-    for n in reversed(range(len(groups))):
-        for total in sums:
-            if n + 1 < len(groups):
-                total.given()
-            total.give(n)
-    for total, out in zip(sums, (w1_o, w2_o)):
-        total.given()
-        for n in range(9):
-            out[n] = obuf[total.w, n * per:(n + 1) * per].reshape(C, C)
+    while not (one.over and two.over):
+        one.advance()
+        two.advance()
     await_sends(0, fields)
     await_sends(1, upstream)
     await_sends(2, hidden)
@@ -577,7 +586,7 @@
         ],
         compiler_params=pltpu.CompilerParams(
             collective_id=0, has_side_effects=True, vmem_limit_bytes=24 * 1024 * 1024),
-    )(fields, upstream, k1, k2)
+    )(fields, upstream, pltpu.with_memory_space_constraint(k1, pltpu.HBM), pltpu.with_memory_space_constraint(k2, pltpu.HBM))
 
 
 def on_device(n_sub, n_t, n_f, fields, upstream, k1, k2):

time: 49.7 us -> 47.2 us (0.950)
  local copies, waits for them, and re-layouts: 4.51 us -> 2.67 us
  Pallas kernels: 42.7 us -> 42.1 us
    unnamed x8 -> x6, local copies, waits for them, and re-layouts: 4.51 us -> 2.67 us
    pallas_call x1, Pallas kernels: 42.7 us -> 42.1 us  [run(): pl.pallas_call(functools.partial(body, n_t, n_f, scale, groups), out_shap...]
where the time goes in v3:
time: 47.2 us; the launch traced here: 47.1 us
  Pallas kernels  42.1 us (89%)
  local copies, waits for them, and re-layouts  2.67 us (6%)
  other arithmetic  1.59 us (3%)
  between operations  0.66 us (1%)
    pallas_call x1, Pallas kernels, run(): pl.pallas_call(functools.partial(body, n_t, n_f, scale, groups), out_shap...  42.1 us
    unnamed x6, local copies, waits for them, and re-layouts  2.67 us

profile of v3, /device:TPU:0, one launch (start us, length us, event | category | flops | bytes accessed | tf_op | source)
XLA Modules:
  0.0 47.1 jit_solution(7657328372452461732)
XLA Ops:
  0.6 0.0 copy-start
  0.6 1.0 %copy.8 = bf16[96,2,2,96]{0,3,2,1:T(8,128)(2,1)S(1)} copy(bf16[96,2,2,96]{3,2,1,0:T(2,128)(2,1)} %param.4) | data formatting | bytes 147456 | tf_op args[0]
  1.7 0.0 copy-done
  1.7 0.1 copy.9
  1.8 42.1 %shard_map.75 = (bf16[2,2,96,96]{3,2,1,0:T(8,128)(2,1)S(1)}, bf16[2,2,96,96]{3,2,1,0:T(8,128)(2,1)S(1)}, bf16[9,96,96]{2,1,0:T(8,128)(2,1)S(1)}, bf16[9,96,96]{2,1,0:T(8,128)(2,1)S(1)}) custom-call(bf16[2,2,96,96]{3,2,1,0:T(8,128)(2,1)S(1)} %bitcast.8, bf16[2,2,96,96]{3,2,1,0:T(8,128)(2,1)S(1)} %bitcast.9, bf16[3,3,96,96]{3,2,1,0:T(8,128)(2,1)} %k1_h.1, ...), custom_call_target="tpu_custom_call" | custom-call | tf_op jit(solution)/shard_map/pallas_call | solution.py:545
  44.0 0.8 %copy.10 = bf16[96,2,2,96]{3,2,1,0:T(2,128)(2,1)} copy(bf16[96,2,2,96]{0,3,2,1:T(8,128)(2,1)S(1)} %bitcast.13) | data formatting | bytes 147456
  44.7 0.8 %copy.11 = bf16[96,2,2,96]{3,2,1,0:T(2,128)(2,1)} copy(bf16[96,2,2,96]{0,3,2,1:T(8,128)(2,1)S(1)} %bitcast.12) | data formatting | bytes 147456
  45.5 0.8 %convert.2 = f32[3,3,96,96]{3,2,1,0:T(8,128)} convert(bf16[3,3,96,96]{3,2,1,0:T(8,128)(2,1)S(1)} %bitcast.11) | non-fusion elementwise | flops 82944 | bytes 497664 | tf_op jit(solution)/shard_map/reshape | solution.py:606
  46.3 0.8 %convert.3 = f32[3,3,96,96]{3,2,1,0:T(8,128)} convert(bf16[3,3,96,96]{3,2,1,0:T(8,128)(2,1)S(1)} %bitcast.10) | non-fusion elementwise | flops 82944 | bytes 497664 | tf_op jit(solution)/shard_map/reshape | solution.py:606
Async XLA Ops:
  0.6 1.1 %copy-start = (bf16[96,2,2,96]{3,2,1,0:T(2,128)(2,1)S(1)}, bf16[96,2,2,96]{3,2,1,0:T(2,128)(2,1)}, u32[]{:S(2)}) copy-start(bf16[96,2,2,96]{3,2,1,0:T(2,128)(2,1)} %param.5) | copy-start | bytes 221188

commit v4 on v3

--- a/solution.py
+++ b/solution.py
@@ -461,13 +461,13 @@
     loads[0].wait()
     loads[1].wait()
     stage(0, fields)
-    stage(1, upstream)
     if blocks > 9 * per:
         for w in range(2):
             acc[w, 9 * per:blocks] = jnp.zeros((blocks - 9 * per, 16, C), F32)
     pl.semaphore_wait(barrier, n_t * n_f - 1)
 
     start(0, fields)
+    stage(1, upstream)
     start(1, upstream)
     loads[2].wait()
     loads[3].wait()
@@ -484,22 +484,22 @@
     stage(3, pre_grad)
     start(3, pre_grad)
     one, two = Sum(0, w1_o), Sum(1, w2_o)
+    cells = flat(hidden)
+    for n in range(9):
+        term = product(cells, xb[n].astype(BF16), 0, 0) * scale
+        acc[1, n * per:(n + 1) * per] = term.reshape(per, 16, C)
+    two.advance()
     weight_terms(xf1, cot, 0)
     one.advance()
+    two.advance()
     one.advance()
     await_arrivals(2, hidden)
     forward_taps(2, hidden, xf2)
-    weight_terms(xf2, flat(upstream), 1)
+    unflat(apply(xf2, k2, 0).astype(BF16), res_o)
     two.advance()
     one.advance()
-    two.advance()
-    unflat(apply(xf2, k2, 0).astype(BF16), res_o)
-    one.advance()
-    two.advance()
     await_arrivals(3, pre_grad)
     backward_taps(3, pre_grad, xb)
-    one.advance()
-    two.advance()
     unflat(apply(xb, k1, 1).astype(BF16), fg_o)
     while not (one.over and two.over):
         one.advance()

time: 47.2 us -> 44.5 us (0.943)
  Pallas kernels: 42.1 us -> 39.4 us
    pallas_call x1, Pallas kernels: 42.1 us -> 39.4 us  [run(): pl.pallas_call(functools.partial(body, n_t, n_f, scale, groups), out_shap...]
where the time goes in v4:
time: 44.5 us; the launch traced here: 44.3 us
  Pallas kernels  39.4 us (89%)
  local copies, waits for them, and re-layouts  2.67 us (6%)
  other arithmetic  1.59 us (4%)
  between operations  0.66 us (1%)
    pallas_call x1, Pallas kernels, run(): pl.pallas_call(functools.partial(body, n_t, n_f, scale, groups), out_shap...  39.4 us
    unnamed x6, local copies, waits for them, and re-layouts  2.67 us

profile of v4, /device:TPU:0, one launch (start us, length us, event | category | flops | bytes accessed | tf_op | source)
XLA Modules:
  0.0 44.3 jit_solution(2806837238087148219)
XLA Ops:
  0.6 0.0 copy-start
  0.6 1.0 %copy.8 = bf16[96,2,2,96]{0,3,2,1:T(8,128)(2,1)S(1)} copy(bf16[96,2,2,96]{3,2,1,0:T(2,128)(2,1)} %param.4) | data formatting | bytes 147456 | tf_op args[0]
  1.7 0.0 copy-done
  1.7 0.1 copy.9
  1.8 39.4 %shard_map.75 = (bf16[2,2,96,96]{3,2,1,0:T(8,128)(2,1)S(1)}, bf16[2,2,96,96]{3,2,1,0:T(8,128)(2,1)S(1)}, bf16[9,96,96]{2,1,0:T(8,128)(2,1)S(1)}, bf16[9,96,96]{2,1,0:T(8,128)(2,1)S(1)}) custom-call(bf16[2,2,96,96]{3,2,1,0:T(8,128)(2,1)S(1)} %bitcast.8, bf16[2,2,96,96]{3,2,1,0:T(8,128)(2,1)S(1)} %bitcast.9, bf16[3,3,96,96]{3,2,1,0:T(8,128)(2,1)} %k1_h.1, ...), custom_call_target="tpu_custom_call" | custom-call | tf_op jit(solution)/shard_map/pallas_call | solution.py:545
  41.2 0.8 %copy.10 = bf16[96,2,2,96]{3,2,1,0:T(2,128)(2,1)} copy(bf16[96,2,2,96]{0,3,2,1:T(8,128)(2,1)S(1)} %bitcast.13) | data formatting | bytes 147456
  42.0 0.8 %copy.11 = bf16[96,2,2,96]{3,2,1,0:T(2,128)(2,1)} copy(bf16[96,2,2,96]{0,3,2,1:T(8,128)(2,1)S(1)} %bitcast.12) | data formatting | bytes 147456
  42.7 0.8 %convert.2 = f32[3,3,96,96]{3,2,1,0:T(8,128)} convert(bf16[3,3,96,96]{3,2,1,0:T(8,128)(2,1)S(1)} %bitcast.11) | non-fusion elementwise | flops 82944 | bytes 497664 | tf_op jit(solution)/shard_map/reshape | solution.py:606
  43.5 0.8 %convert.3 = f32[3,3,96,96]{3,2,1,0:T(8,128)} convert(bf16[3,3,96,96]{3,2,1,0:T(8,128)(2,1)S(1)} %bitcast.10) | non-fusion elementwise | flops 82944 | bytes 497664 | tf_op jit(solution)/shard_map/reshape | solution.py:606
Async XLA Ops:
  0.6 1.1 %copy-start = (bf16[96,2,2,96]{3,2,1,0:T(2,128)(2,1)S(1)}, bf16[96,2,2,96]{3,2,1,0:T(2,128)(2,1)}, u32[]{:S(2)}) copy-start(bf16[96,2,2,96]{3,2,1,0:T(2,128)(2,1)} %param.5) | copy-start | bytes 221188
